TPU v7x, 32 devices: a whole 2x2x4 slice. The times are simulated.
32 devices in a mesh: group: 4 (over x, core), tensor: 4 (over z), dp: 2 (over y).
Axes of the slice: x: 2, y: 2, z: 4, core: 2. Of those that a mesh axis runs over, the one named last changes fastest.
Arguments:
- doc_emb: bfloat16 [48, 4096], P('group', 'dp'), may hold values from -6 to 6
- row_emb: bfloat16 [64, 4096], P(None, 'dp'), may hold values from -6 to 6
- hyper_in: bfloat16 [4096, 8192], P('dp', 'tensor'), may hold values from -0.09375 to 0.09375
- hyper_out: bfloat16 [8192, 8192], P('tensor', 'dp'), may hold values from -0.0625 to 0.0625
- assign: int32 [48], replicated, may hold values from 0 to 47, each once
- states: bfloat16 [2304, 8192], P('group', 'tensor'), may hold values from -6 to 6
- proj_weight: bfloat16 [8192, 8192], P('tensor', 'dp'), may hold values from -0.0625 to 0.0625
- targets: bfloat16 [2304, 8192], P(('group', 'tensor'), 'dp'), may hold values from -6 to 6
Outputs:
- adapted: bfloat16 [2304, 8192], P(('group', 'tensor'), 'dp')
- grad_down: float32 [48, 32, 8192], P('group', None, 'tensor')
- grad_up: float32 [48, 32, 8192], P('group', None, ('dp', 'tensor'))
Inputs may be any that keep to these rules, and one draw needn't show every extreme that they name: `assign`: every document is named by exactly one slot.
All inputs are finite; a program needn't handle non-finite values.
Results may differ from a plain program's by a relative error of at most 0.02.
Values may be sent and summed in bfloat16 or wider, within the bound.
No kernel may reach another device: no remote copies, remote signals or barrier semaphores. Data moves between devices by JAX's collectives and lax.ppermute only.
A program may use at most 128 MiB of HBM per device.

v0:
```python
import math
import jax
import jax.numpy as jnp
from jax import lax
from jax.sharding import PartitionSpec as P

D = 8192
R = 32
LOWDIM_MULTIPLE = 0.1


def spread(block, axis, owner):
    block = jnp.where(lax.axis_index(axis) == owner, block, jnp.zeros_like(block))
    return lax.psum(block, axis)


def hypernet(doc_rows, row_emb, hyper_in, hyper_out):
    doc_count = doc_rows.shape[0]
    pre_doc, pre_row = (
        lax.psum(
            jnp.dot(doc_rows, hyper_in, preferred_element_type=jnp.float32).astype(jnp.bfloat16),
            "dp",
        ).astype(jnp.float32),
        lax.psum(
            jnp.dot(row_emb, hyper_in, preferred_element_type=jnp.float32).astype(jnp.bfloat16),
            "dp",
        ).astype(jnp.float32),
    )
    hidden = jax.nn.silu(pre_doc[:, None, :] + pre_row[None, :, :]).astype(jnp.bfloat16)
    hidden = hidden.reshape(doc_count * 2 * R, hidden.shape[2])
    partial_value = jnp.dot(hidden, hyper_out, preferred_element_type=jnp.float32)
    summed = lax.psum(partial_value.astype(jnp.bfloat16), "tensor")
    factors = summed.reshape(doc_count, 2 * R, hyper_out.shape[1])
    ratio_axes = lax.axis_size("tensor") // lax.axis_size("dp")
    owner_rows = spread(factors[:, :R, :], "dp", lax.axis_index("tensor") // ratio_axes)
    col_width = hyper_out.shape[1] // ratio_axes
    down_block = lax.dynamic_slice_in_dim(
        owner_rows, lax.axis_index("tensor") % ratio_axes * col_width, col_width, 2
    )
    return (down_block, factors[:, R:, :])


def body(doc_emb, row_emb, hyper_in, hyper_out, assign, states, proj_weight, targets):
    doc_count = doc_emb.shape[0]
    group_start = lax.axis_index("group") * doc_count
    slot_docs = lax.dynamic_slice_in_dim(assign, group_start, doc_count)
    everyone = lax.all_gather(doc_emb, "group", axis=0, tiled=True)
    picker = (slot_docs[:, None] == jnp.arange(everyone.shape[0], dtype=jnp.int32)[None, :]).astype(
        jnp.bfloat16
    )
    chosen = jnp.dot(picker, everyone, preferred_element_type=jnp.float32).astype(jnp.bfloat16)
    slot_down, slot_up_factor = hypernet(chosen, row_emb, hyper_in, hyper_out)
    token_count = states.shape[0]
    per_doc = token_count // doc_count
    fan_width_multiplier = 1.0 / math.sqrt(D)
    bundled_entries = states.reshape(doc_count, per_doc, states.shape[1])
    low_part = jnp.einsum(
        "quw,qlw->qul", bundled_entries, slot_down, preferred_element_type=jnp.float32
    ).reshape(token_count, R)
    base_part = jnp.dot(states, proj_weight, preferred_element_type=jnp.float32)
    frozen_output, low_sum = (
        lax.psum_scatter(
            base_part.astype(jnp.bfloat16), "tensor", scatter_dimension=0, tiled=True
        ).astype(jnp.float32),
        lax.psum_scatter(
            low_part.astype(jnp.bfloat16), "tensor", scatter_dimension=0, tiled=True
        ).astype(jnp.float32),
    )
    row_count = frozen_output.shape[0]
    row_start = lax.axis_index("tensor") * row_count
    owner_doc = (row_start + jnp.arange(row_count, dtype=jnp.int32)) // per_doc
    document_member = owner_doc[:, None] == jnp.arange(doc_count, dtype=jnp.int32)[None, :]
    narrow_basis_map = (low_sum * fan_width_multiplier).astype(jnp.bfloat16)
    broadcast_rows = jnp.where(
        document_member[:, :, None], narrow_basis_map[:, None, :], jnp.zeros((), jnp.bfloat16)
    ).reshape(row_count, doc_count * R)
    up_factor_rows = slot_up_factor.reshape(doc_count * R, slot_up_factor.shape[2])
    raised_rows = frozen_output + LOWDIM_MULTIPLE * jnp.dot(
        broadcast_rows, up_factor_rows, preferred_element_type=jnp.float32
    )
    adapted = raised_rows.astype(jnp.bfloat16)
    residual = (raised_rows - targets.astype(jnp.float32)).astype(jnp.bfloat16)
    partial_up_gradient = LOWDIM_MULTIPLE * lax.dot_general(
        broadcast_rows, residual, (((0,), (0,)), ((), ())), preferred_element_type=jnp.float32
    )
    grad_up_local = lax.psum_scatter(
        partial_up_gradient.reshape(doc_count, R, up_factor_rows.shape[1]).astype(jnp.bfloat16),
        "tensor",
        scatter_dimension=2,
        tiled=True,
    ).astype(jnp.float32)
    document_list = lax.dot_general(
        residual, up_factor_rows, (((1,), (1,)), ((), ())), preferred_element_type=jnp.float32
    ).reshape(row_count, doc_count, R)
    token_portion = LOWDIM_MULTIPLE * jnp.sum(
        jnp.where(document_member[:, :, None], document_list, 0.0), axis=1
    )
    placed = lax.dynamic_update_slice_in_dim(
        jnp.zeros((token_count, R), jnp.float32), token_portion, row_start, 0
    )
    position_sensitivity = lax.psum(placed, ("tensor", "dp")).astype(jnp.bfloat16)
    lowering_matrix_sensitivity = fan_width_multiplier * jnp.einsum(
        "oed,oec->odc",
        position_sensitivity.reshape(doc_count, per_doc, R),
        bundled_entries,
        preferred_element_type=jnp.float32,
    )
    own_docs = group_start + jnp.arange(doc_count, dtype=jnp.int32)
    initial_grads = (
        jnp.zeros(
            (
                doc_count,
                lowering_matrix_sensitivity.shape[1] * lowering_matrix_sensitivity.shape[2],
            ),
            jnp.float32,
        ),
        jnp.zeros((doc_count, grad_up_local.shape[1] * grad_up_local.shape[2]), jnp.float32),
    )
    pieces = (
        lax.all_gather(
            lowering_matrix_sensitivity.astype(jnp.bfloat16), "group", axis=0, tiled=True
        ).astype(jnp.float32),
        lax.all_gather(grad_up_local.astype(jnp.bfloat16), "group", axis=0, tiled=True).astype(
            jnp.float32
        ),
    )
    piece_rows = pieces[0].shape[0]
    picker = (own_docs[:, None] == assign[None, :]).astype(jnp.float32)
    first = initial_grads[0] + jnp.dot(
        picker, pieces[0].reshape(piece_rows, -1), precision=lax.Precision.HIGHEST
    )
    second = initial_grads[1] + jnp.dot(
        picker, pieces[1].reshape(piece_rows, -1), precision=lax.Precision.HIGHEST
    )
    grad_down = first.reshape(lowering_matrix_sensitivity.shape)
    grad_up = second.reshape(grad_up_local.shape)
    return (adapted, grad_down, grad_up)


def solution(mesh):
    in_specs = (
        P("group", "dp"),
        P(None, "dp"),
        P("dp", "tensor"),
        P("tensor", "dp"),
        P(),
        P("group", "tensor"),
        P("tensor", "dp"),
        P(("group", "tensor"), "dp"),
    )
    out_specs = (
        P(("group", "tensor"), "dp"),
        P("group", None, "tensor"),
        P("group", None, ("dp", "tensor")),
    )
    return jax.shard_map(body, mesh=mesh, in_specs=in_specs, out_specs=out_specs, check_vma=False)
```

profile of v0, /device:TPU:0, one launch (start us, length us, event | category | flops | bytes accessed | tf_op | source)
XLA Modules:
  0.0 643.9 jit_solution(16494009230367694234)
XLA Ops:
  7.2 5.9 convolution_convert_fusion.2
  13.2 7.2 %all-gather = bf16[4,12,2048]{2,1,0:T(8,128)(2,1)S(1)} all-gather(bf16[1,12,2048]{2,1,0:T(8,128)(2,1)S(1)} %bitcast.83), channel_id=1, replica_groups=mesh['group'=4,'tensor'=4,'dp'=2] {'group'}, dimensions={0}, use_global_device_ids=true | all-gather | bytes 245760 | tf_op jit(solution)/shard_map/all_gather | solution.py:47
  20.6 4.8 convolution_convert_fusion.4
  25.4 8.9 %psum.35 = bf16[12,2048]{1,0:T(8,128)(2,1)S(1)} all-reduce(bf16[12,2048]{1,0:T(8,128)(2,1)S(1)} %convolution_convert_fusion.4), channel_id=1, replica_groups=mesh['group'=4,'tensor'=4,'dp'=2] {'dp'}, use_global_device_ids=true, to_apply=%region_1.0 | all-reduce | flops 24576 | bytes 98304 | tf_op jit(solution)/shard_map/psum | solution.py:20
  34.3 5.0 all-reduce.4.cloned.1.call-done
  39.3 1.0 convert_element_type.76
  40.3 0.8 broadcast_add_fusion
  41.1 1.7 fusion.6
  42.8 18.5 %convolution_convert_fusion = bf16[768,4096]{1,0:T(8,128)(2,1)} fusion(bf16[768,2048]{1,0:T(8,128)(2,1)S(1)} %fusion.6, bf16[2048,4096]{1,0:T(8,128)(2,1)} %param.11), kind=kOutput, calls=%fused_computation | convolution fusion | flops 12888047616 | bytes 26214400 | tf_op jit(solution)/shard_map/dot_general | solution.py:31
  61.4 222.9 %all-reduce.6.cloned.1.call-done = bf16[12,64,4096]{2,1,0:T(8,128)(2,1)} async-done(((bf16[12,64,4096]{2,1,0:T(8,128)(2,1)}), bf16[12,64,4096]{2,1,0:T(8,128)(2,1)}) %all-reduce.6.cloned.1.call-update) | async-done | bytes 6291472 | tf_op jit(solution)/shard_map/psum | solution.py:32
  284.4 3.8 slice_select_fusion
  288.2 84.8 %all-reduce.8.cloned.1.call-done = bf16[12,32,4096]{2,1,0:T(8,128)(2,1)} async-done(((bf16[12,32,4096]{2,1,0:T(8,128)(2,1)}), bf16[12,32,4096]{2,1,0:T(8,128)(2,1)}) %all-reduce.8.cloned.1.call-update) | async-done | bytes 3145744 | tf_op jit(solution)/shard_map/psum | solution.py:14
  373.0 2.1 fusion.31
  375.2 0.8 copy.27
  376.2 15.0 %convolution_convert_fusion.1 = bf16[576,4096]{1,0:T(8,128)(2,1)} fusion(bf16[576,2048]{1,0:T(8,128)(2,1)S(1)} %copy-done, bf16[2048,4096]{1,0:T(8,128)(2,1)} %param.14), kind=kOutput, calls=%fused_computation.11 | convolution fusion | flops 9666035712 | bytes 23855104 | tf_op jit(solution)/shard_map/dot_general | solution.py:60
  391.3 4.4 reduce-scatter.10.cloned.1.call-done
  395.7 0.8 copy.26
  396.5 0.7 broadcast_select_fusion
  397.2 84.1 %reduce-scatter.6.cloned.1.call-done = bf16[144,4096]{1,0:T(8,128)(2,1)} async-done(((bf16[576,4096]{1,0:T(8,128)(2,1)}), bf16[144,4096]{1,0:T(8,128)(2,1)}) %reduce-scatter.6.cloned.1.call-update) | async-done | bytes 1179664 | tf_op jit(solution)/shard_map/reduce_scatter | solution.py:62
  481.4 4.1 fusion.47
  485.5 2.7 multiply_convert_fusion
  488.2 0.6 copy-done.6
  488.8 3.6 fusion.23
  492.9 40.6 %psum.39 = bf16[576,32]{0,1:T(8,128)(2,1)S(1)} all-reduce(f32[576,32]{0,1:T(8,128)S(1)} %dynamic_update_slice.3), channel_id=1, replica_groups=mesh['group'=4,'tensor'=4,'dp'=2] {'tensor','dp'}, use_global_device_ids=true, to_apply=%region_7.8 | all-reduce | flops 18432 | bytes 110592 | tf_op jit(solution)/shard_map/psum | solution.py:101
  533.7 1.7 multiply_convert_fusion.1
  535.7 15.1 %reduce-scatter.8.cloned.1.call-done = bf16[12,32,1024]{2,1,0:T(8,128)(2,1)} async-done(((bf16[12,32,4096]{2,1,0:T(8,128)(2,1)}), bf16[12,32,1024]{2,1,0:T(8,128)(2,1)}) %reduce-scatter.8.cloned.1.call-update) | async-done | bytes 786448 | tf_op jit(solution)/shard_map/reduce_scatter | solution.py:86
  550.8 48.7 %all-gather.4.cloned.1.call-done = bf16[48,32,2048]{2,1,0:T(8,128)(2,1)} async-done(((bf16[12,32,2048]{2,1,0:T(8,128)(2,1)}), bf16[48,32,2048]{2,1,0:T(8,128)(2,1)}) %all-gather.4.cloned.1.call-update) | async-done | bytes 6291472 | tf_op jit(solution)/shard_map/all_gather | solution.py:120
  599.6 9.6 %fusion = f32[12,32,2048]{2,0,1:T(8,128)S(1)} fusion(s32[48]{0:T(128)S(1)} %copy-done.8, s32[12]{0:T(128)S(1)} %iota_add_fusion, bf16[6,8,32,2048]{3,2,1,0:T(8,128)(2,1)} %bitcast.79), kind=kOutput, calls=%fused_computation.1 | convolution fusion | flops 75498048 | bytes 9437424 | tf_op jit(solution)/shard_map/dot_general | solution.py:129
  609.1 3.5 copy.23
  612.6 17.1 %all-gather.6.cloned.1.call-done = bf16[48,32,1024]{2,1,0:T(8,128)(2,1)} async-done(((bf16[12,32,1024]{2,1,0:T(8,128)(2,1)}), bf16[48,32,1024]{2,1,0:T(8,128)(2,1)}) %all-gather.6.cloned.1.call-update) | async-done | bytes 3145744 | tf_op jit(solution)/shard_map/all_gather | solution.py:123
  629.7 5.3 fusion.9
  635.0 2.1 copy.24
  (44 shorter events, 1.7 us)
Async XLA Ops:
  7.2 365.9 %copy-start = (bf16[576,2048]{1,0:T(8,128)(2,1)S(1)}, bf16[576,2048]{1,0:T(8,128)(2,1)}, u32[]{:S(2)}) copy-start(bf16[576,2048]{1,0:T(8,128)(2,1)} %param.13) | copy-start | bytes 7077892
  7.2 6.0 copy-start.4
  7.2 13.3 %copy-start.7 = (s32[48]{0:T(128)S(1)}, s32[48]{0:T(128)}, u32[]{:S(2)}) copy-start(s32[48]{0:T(128)} %param.12) | copy-start | bytes 580
  7.2 32.1 %all-reduce.4.cloned.1.call-start = ((), (), s32[]{:S(2)}) async-start(), calls=%async_computation.4 | async-start | bytes 524288 | tf_op jit(solution)/shard_map/psum | solution.py:24
  13.2 271.2 %all-reduce.6.cloned.1.call-start = ((), (), s32[]{:S(2)}) async-start(), calls=%async_computation.5 | async-start | bytes 12582912 | tf_op jit(solution)/shard_map/psum | solution.py:32
  61.4 311.7 %all-reduce.8.cloned.1.call-start = ((), (), s32[]{:S(2)}) async-start(), calls=%async_computation.6 | async-start | bytes 6291456 | tf_op jit(solution)/shard_map/psum | solution.py:14
  288.1 107.5 %reduce-scatter.10.cloned.1.call-start = ((), (), s32[]{:S(2)}) async-start(), calls=%async_computation.10 | async-start | bytes 184320
  376.0 105.4 %reduce-scatter.6.cloned.1.call-start = ((), (), s32[]{:S(2)}) async-start(), calls=%async_computation.3 | async-start | bytes 5898240 | tf_op jit(solution)/shard_map/reduce_scatter | solution.py:62
  391.2 159.6 %reduce-scatter.8.cloned.1.call-start = ((), (), s32[]{:S(2)}) async-start(), calls=%async_computation.8 | async-start | bytes 3932160 | tf_op jit(solution)/shard_map/reduce_scatter | solution.py:86
  391.3 5.3 copy-start.5
  397.2 88.2 %copy-start.2 = (bf16[144,4096]{1,0:T(8,128)(2,1)S(1)}, bf16[144,4096]{1,0:T(8,128)(2,1)}, u32[]{:S(2)}) copy-start(bf16[144,4096]{1,0:T(8,128)(2,1)} %param.15) | copy-start | bytes 3538948
  481.4 4.1 copy-start.3
  485.5 2.7 copy-start.1
  488.2 0.7 copy-start.6
  488.2 111.4 %all-gather.4.cloned.1.call-start = ((), (), s32[]{:S(2)}) async-start(), calls=%async_computation.7 | async-start | bytes 7864320 | tf_op jit(solution)/shard_map/all_gather | solution.py:120
  533.7 65.9 %copy-start.8 = (s32[48]{0:T(128)S(1)}, s32[48]{0:T(128)}, u32[]{:S(2)}) copy-start(s32[48]{0:T(128)} %param.12) | copy-start | bytes 580
  535.4 94.2 %all-gather.6.cloned.1.call-start = ((), (), s32[]{:S(2)}) async-start(), calls=%async_computation.9 | async-start | bytes 3932160 | tf_op jit(solution)/shard_map/all_gather | solution.py:123
Sparse Core Ops, SparseCore 0:
  13.3 26.0 all-reduce.3
  61.5 222.8 all-reduce.5
  288.3 84.7 all-reduce.7
  376.1 19.5 reduce-scatter.9
  397.8 83.4 reduce-scatter.5
  488.3 62.4 reduce-scatter.7
  552.9 46.5 all-gather.3
  601.1 28.4 all-gather.5
where the time goes:
time: 644 us
  waiting for transfers between devices  482 us (75%)
  matrix products  73.3 us (11%)
  blocking collectives  56.7 us (9%)
  between operations  14.4 us (2%)
  local copies, waits for them, and re-layouts  8.55 us (1%)
  other arithmetic  7.99 us (1%)
    psum x1, waiting for transfers between devices, hypernet(): summed = lax.psum(partial_value.astype(jnp.bfloat16), 'tensor')  223 us
    psum x1, waiting for transfers between devices, spread(): return lax.psum(block, axis)  84.8 us
    reduce_scatter x1, waiting for transfers between devices, body(): lax.psum_scatter(base_part.astype(jnp.bfloat16), 'tensor', scatter_dimens...  84.1 us
    all_gather x1, waiting for transfers between devices, body(): lax.all_gather(lowering_matrix_sensitivity.astype(jnp.bfloat16), 'group',...  48.7 us
    psum x1, blocking collectives, body(): lax.psum(placed, ('tensor', 'dp')).astype(jnp.bfloat16)  40.6 us
    dot_general x1, matrix products, hypernet(): jnp.dot(hidden, hyper_out, preferred_element_type=jnp.float32)  18.5 us
    all_gather x1, waiting for transfers between devices, body(): lax.all_gather(grad_up_local.astype(jnp.bfloat16), 'group', axis=0, tiled...  17.1 us
    reduce_scatter x1, waiting for transfers between devices, body(): lax.psum_scatter(partial_up_gradient.reshape(doc_count, R, up_factor_rows...  15.1 us
  transfers between devices with their start and end apart: 8, of which 8 were waited for; matrix products, arithmetic and copies ran while one was open for 6% of the time, Pallas kernels for 0%

commit v1 on v0

--- a/solution.py
+++ b/solution.py
@@ -7,6 +7,15 @@
 D = 8192
 R = 32
 LOWDIM_MULTIPLE = 0.1
+
+
+def use_bench(xx):
+    return jnp.concatenate(
+        lax.all_to_all(
+            jnp.stack([xx] * lax.axis_size("group")), axis_name="group", split_axis=0, concat_axis=0
+        ),
+        axis=0,
+    )
 
 
 def spread(block, axis, owner):
@@ -117,9 +126,7 @@
         jnp.zeros((doc_count, grad_up_local.shape[1] * grad_up_local.shape[2]), jnp.float32),
     )
     pieces = (
-        lax.all_gather(
-            lowering_matrix_sensitivity.astype(jnp.bfloat16), "group", axis=0, tiled=True
-        ).astype(jnp.float32),
+        use_bench(lowering_matrix_sensitivity.astype(jnp.bfloat16)).astype(jnp.float32),
         lax.all_gather(grad_up_local.astype(jnp.bfloat16), "group", axis=0, tiled=True).astype(
             jnp.float32
         ),

time: 644 us -> 658 us (1.022)
  waiting for transfers between devices: 482 us -> 489 us
    all_to_all x0 -> x1, waiting for transfers between devices: none -> 79.8 us  [use_bench(): lax.all_to_all(jnp.stack([xx] * lax.axis_size('group')), axis_name='group...]
    all_gather x1 -> x0, waiting for transfers between devices: 48.7 us -> none  [body(): lax.all_gather(lowering_matrix_sensitivity.astype(jnp.bfloat16), 'group',...]
    all_gather x1, waiting for transfers between devices: 17.1 us -> 0.01 us  [body(): lax.all_gather(grad_up_local.astype(jnp.bfloat16), 'group', axis=0, tiled...]
    reduce_scatter x1, waiting for transfers between devices: 15.1 us -> 7.43 us  [body(): lax.psum_scatter(partial_up_gradient.reshape(doc_count, R, up_factor_rows...]
  transfers between devices with their start and end apart: 8 -> 8, of which waited for: 8 -> 7; matrix products, arithmetic and copies ran while one was open for 6% -> 6% of each run, Pallas kernels for 0% -> 0%
where the time goes in v1:
time: 658 us
  waiting for transfers between devices  489 us (74%)
  matrix products  72.1 us (11%)
  blocking collectives  56.7 us (9%)
  between operations  14.4 us (2%)
  local copies, waits for them, and re-layouts  12 us (2%)
  other arithmetic  7.99 us (1%)
    psum x1, waiting for transfers between devices, hypernet(): summed = lax.psum(partial_value.astype(jnp.bfloat16), 'tensor')  223 us
    psum x1, waiting for transfers between devices, spread(): return lax.psum(block, axis)  84.8 us
    reduce_scatter x1, waiting for transfers between devices, body(): lax.psum_scatter(base_part.astype(jnp.bfloat16), 'tensor', scatter_dimens...  84.1 us
    all_to_all x1, waiting for transfers between devices, use_bench(): lax.all_to_all(jnp.stack([xx] * lax.axis_size('group')), axis_name='group...  79.8 us
    psum x1, blocking collectives, body(): lax.psum(placed, ('tensor', 'dp')).astype(jnp.bfloat16)  40.6 us
    dot_general x1, matrix products, hypernet(): jnp.dot(hidden, hyper_out, preferred_element_type=jnp.float32)  18.5 us
    dot_general x1, matrix products, body(): base_part = jnp.dot(states, proj_weight, preferred_element_type=jnp.float32)  15 us
  transfers between devices with their start and end apart: 8, of which 7 were waited for; matrix products, arithmetic and copies ran while one was open for 6% of the time, Pallas kernels for 0%

profile of v1, /device:TPU:0, one launch (start us, length us, event | category | flops | bytes accessed | tf_op | source)
XLA Modules:
  0.0 657.8 jit_solution(17882291807797755330)
XLA Ops:
  7.2 5.9 convolution_convert_fusion.2
  13.2 7.2 %all-gather = bf16[4,12,2048]{2,1,0:T(8,128)(2,1)S(1)} all-gather(bf16[1,12,2048]{2,1,0:T(8,128)(2,1)S(1)} %bitcast.83), channel_id=1, replica_groups=mesh['group'=4,'tensor'=4,'dp'=2] {'group'}, dimensions={0}, use_global_device_ids=true | all-gather | bytes 245760 | tf_op jit(solution)/shard_map/all_gather | solution.py:56
  20.6 4.8 convolution_convert_fusion.4
  25.4 8.9 %psum.35 = bf16[12,2048]{1,0:T(8,128)(2,1)S(1)} all-reduce(bf16[12,2048]{1,0:T(8,128)(2,1)S(1)} %convolution_convert_fusion.4), channel_id=1, replica_groups=mesh['group'=4,'tensor'=4,'dp'=2] {'dp'}, use_global_device_ids=true, to_apply=%region_1.0 | all-reduce | flops 24576 | bytes 98304 | tf_op jit(solution)/shard_map/psum | solution.py:29
  34.3 5.0 all-reduce.4.cloned.1.call-done
  39.3 1.0 convert_element_type.76
  40.3 0.8 broadcast_add_fusion
  41.1 1.7 fusion.6
  42.8 18.5 %convolution_convert_fusion = bf16[768,4096]{1,0:T(8,128)(2,1)} fusion(bf16[768,2048]{1,0:T(8,128)(2,1)S(1)} %fusion.6, bf16[2048,4096]{1,0:T(8,128)(2,1)} %param.11), kind=kOutput, calls=%fused_computation | convolution fusion | flops 12888047616 | bytes 26214400 | tf_op jit(solution)/shard_map/dot_general | solution.py:40
  61.4 222.9 %all-reduce.6.cloned.1.call-done = bf16[12,64,4096]{2,1,0:T(8,128)(2,1)} async-done(((bf16[12,64,4096]{2,1,0:T(8,128)(2,1)}), bf16[12,64,4096]{2,1,0:T(8,128)(2,1)}) %all-reduce.6.cloned.1.call-update) | async-done | bytes 6291472 | tf_op jit(solution)/shard_map/psum | solution.py:41
  284.3 3.8 slice_select_fusion
  288.2 84.8 %all-reduce.8.cloned.1.call-done = bf16[12,32,4096]{2,1,0:T(8,128)(2,1)} async-done(((bf16[12,32,4096]{2,1,0:T(8,128)(2,1)}), bf16[12,32,4096]{2,1,0:T(8,128)(2,1)}) %all-reduce.8.cloned.1.call-update) | async-done | bytes 3145744 | tf_op jit(solution)/shard_map/psum | solution.py:23
  373.0 2.1 fusion.31
  375.2 0.8 copy.27
  376.2 15.0 %convolution_convert_fusion.1 = bf16[576,4096]{1,0:T(8,128)(2,1)} fusion(bf16[576,2048]{1,0:T(8,128)(2,1)S(1)} %copy-done, bf16[2048,4096]{1,0:T(8,128)(2,1)} %param.14), kind=kOutput, calls=%fused_computation.11 | convolution fusion | flops 9666035712 | bytes 23855104 | tf_op jit(solution)/shard_map/dot_general | solution.py:69
  391.3 4.4 reduce-scatter.10.cloned.1.call-done
  395.7 0.8 copy.26
  396.5 0.7 broadcast_select_fusion
  397.2 84.1 %reduce-scatter.6.cloned.1.call-done = bf16[144,4096]{1,0:T(8,128)(2,1)} async-done(((bf16[576,4096]{1,0:T(8,128)(2,1)}), bf16[144,4096]{1,0:T(8,128)(2,1)}) %reduce-scatter.6.cloned.1.call-update) | async-done | bytes 1179664 | tf_op jit(solution)/shard_map/reduce_scatter | solution.py:71
  481.3 4.1 fusion.47
  485.4 2.7 multiply_convert_fusion
  488.1 0.7 copy-done.6
  488.8 3.6 fusion.23
  492.9 40.6 %psum.39 = bf16[576,32]{0,1:T(8,128)(2,1)S(1)} all-reduce(f32[576,32]{0,1:T(8,128)S(1)} %dynamic_update_slice.3), channel_id=1, replica_groups=mesh['group'=4,'tensor'=4,'dp'=2] {'tensor','dp'}, use_global_device_ids=true, to_apply=%region_7.8 | all-reduce | flops 18432 | bytes 110592 | tf_op jit(solution)/shard_map/psum | solution.py:110
  534.2 3.4 stack.2
  537.6 5.4 all-to-all-start
  543.3 7.4 %reduce-scatter.8.cloned.1.call-done = bf16[12,32,1024]{2,1,0:T(8,128)(2,1)} async-done(((bf16[12,32,4096]{2,1,0:T(8,128)(2,1)}), bf16[12,32,1024]{2,1,0:T(8,128)(2,1)}) %reduce-scatter.8.cloned.1.call-update) | async-done | bytes 786448 | tf_op jit(solution)/shard_map/reduce_scatter | solution.py:95
  550.7 79.8 %all-to-all-done = bf16[4,12,32,2048]{3,2,1,0:T(8,128)(2,1)} async-done(((bf16[4,12,32,2048]{3,2,1,0:T(8,128)(2,1)}), bf16[4,12,32,2048]{3,2,1,0:T(8,128)(2,1)}, u32[]{:S(2)}, u32[]{:S(2)}) %all-to-all-start) | async-done | bytes 6291488 | tf_op jit(solution)/shard_map/all_to_all | solution.py:14
  630.5 9.6 %fusion = f32[12,32,2048]{2,0,1:T(8,128)S(1)} fusion(s32[48]{0:T(128)S(1)} %copy-done.8, s32[12]{0:T(128)S(1)} %iota_add_fusion, bf16[6,8,32,2048]{3,2,1,0:T(8,128)(2,1)} %bitcast.20), kind=kOutput, calls=%fused_computation.1 | convolution fusion | flops 75498048 | bytes 9437424 | tf_op jit(solution)/shard_map/dot_general | solution.py:136
  640.1 3.5 copy.23
  643.6 5.3 fusion.9
  648.9 2.1 copy.24
  (44 shorter events, 2.2 us)
Async XLA Ops:
  7.2 365.8 %copy-start = (bf16[576,2048]{1,0:T(8,128)(2,1)S(1)}, bf16[576,2048]{1,0:T(8,128)(2,1)}, u32[]{:S(2)}) copy-start(bf16[576,2048]{1,0:T(8,128)(2,1)} %param.13) | copy-start | bytes 7077892
  7.2 6.0 copy-start.4
  7.2 13.3 %copy-start.7 = (s32[48]{0:T(128)S(1)}, s32[48]{0:T(128)}, u32[]{:S(2)}) copy-start(s32[48]{0:T(128)} %param.12) | copy-start | bytes 580
  7.2 32.1 %all-reduce.4.cloned.1.call-start = ((), (), s32[]{:S(2)}) async-start(), calls=%async_computation.5 | async-start | bytes 524288 | tf_op jit(solution)/shard_map/psum | solution.py:33
  13.2 271.2 %all-reduce.6.cloned.1.call-start = ((), (), s32[]{:S(2)}) async-start(), calls=%async_computation.6 | async-start | bytes 12582912 | tf_op jit(solution)/shard_map/psum | solution.py:41
  61.3 311.7 %all-reduce.8.cloned.1.call-start = ((), (), s32[]{:S(2)}) async-start(), calls=%async_computation.7 | async-start | bytes 6291456 | tf_op jit(solution)/shard_map/psum | solution.py:23
  288.1 107.5 %reduce-scatter.10.cloned.1.call-start = ((), (), s32[]{:S(2)}) async-start(), calls=%async_computation.10 | async-start | bytes 184320
  376.0 105.3 %reduce-scatter.6.cloned.1.call-start = ((), (), s32[]{:S(2)}) async-start(), calls=%async_computation.4 | async-start | bytes 5898240 | tf_op jit(solution)/shard_map/reduce_scatter | solution.py:71
  391.2 159.5 %reduce-scatter.8.cloned.1.call-start = ((), (), s32[]{:S(2)}) async-start(), calls=%async_computation.8 | async-start | bytes 3932160 | tf_op jit(solution)/shard_map/reduce_scatter | solution.py:95
  391.3 5.3 copy-start.5
  397.2 88.2 %copy-start.2 = (bf16[144,4096]{1,0:T(8,128)(2,1)S(1)}, bf16[144,4096]{1,0:T(8,128)(2,1)}, u32[]{:S(2)}) copy-start(bf16[144,4096]{1,0:T(8,128)(2,1)} %param.15) | copy-start | bytes 3538948
  481.3 4.1 copy-start.3
  485.4 2.7 copy-start.1
  488.1 0.7 copy-start.6
  537.6 92.9 %copy-start.8 = (s32[48]{0:T(128)S(1)}, s32[48]{0:T(128)}, u32[]{:S(2)}) copy-start(s32[48]{0:T(128)} %param.12) | copy-start | bytes 580
  537.6 92.9 %all-to-all-start = ((bf16[4,12,32,2048]{3,2,1,0:T(8,128)(2,1)}), bf16[4,12,32,2048]{3,2,1,0:T(8,128)(2,1)}, u32[]{:S(2)}, u32[]{:S(2)}) async-start(bf16[4,12,32,2048]{3,2,1,0:T(8,128)(2,1)} %stack.2), calls=%async_computation.1 | async-start | bytes 12582912 | tf_op jit(solution)/shard_map/all_to_all | solution.py:14
  543.0 100.6 %all-gather.3.cloned.1.call-start = ((), (), s32[]{:S(2)}) async-start(), calls=%async_computation.9 | async-start | bytes 3932160 | tf_op jit(solution)/shard_map/all_gather | solution.py:130
Sparse Core Ops, SparseCore 0:
  13.3 26.0 all-reduce.3
  61.5 222.8 all-reduce.5
  288.3 84.7 all-reduce.7
  376.1 19.5 reduce-scatter.9
  397.8 83.4 reduce-scatter.5
  488.3 62.4 reduce-scatter.7
  552.3 45.7 all-gather.2
